TPU v7x, 128 devices: a whole 4x4x4 slice. The times are simulated.
128 devices in a mesh: batch: 2 (over x_hi), space: 64 (over z, y, x_lo, core).
Axes of the slice: x: 4 (x_hi: 2, x_lo: 2; x = x_hi * 2 + x_lo), y: 4, z: 4, core: 2. Of those that a mesh axis runs over, the one named last changes fastest.
Arguments:
- courant: float32 [512, 16, 256], P('space'), may hold values from 0.06 to 0.18
- wavelet: float32 [2, 256, 7], P('batch'), may hold values from -6 to 6
- source_owner: int32 [2, 256], P('batch'), may hold values from 0 to 63
- source_cell: int32 [2, 256], P('batch'), may hold values from 0 to 32767
- traces: float32 [2, 16384, 7], P('batch', 'space'), may hold values from -6 to 6
- station_owner: int32 [2, 16384, 1], P('batch', 'space'), may hold values from 0 to 63; in each aligned block of 256 rows (0 to 255, 256 to 511, ..., all dimensions but the last counted through in order) at most 8 rows name the same one
- station_cell: int32 [2, 16384], P('batch', 'space'), may hold values from 0 to 32767
Outputs:
- update: float32 [512, 16, 256], P('space', 'batch')
- agreement: float32 [1], replicated
Inputs may be any that keep to these rules, and one draw needn't show every extreme that they name: `station_owner`: among the 256 trace rows of one device, at most 8 name the same owner, and in every draw some device reaches 8 for some owner.
All inputs are finite; a program needn't handle non-finite values.
Results may differ from a plain program's by a relative error of at most 0.0003.
Values sent between devices are 32-bit elements; how exact they have to be, the bound alone decides.
No kernel may reach another device: no remote copies, remote signals or barrier semaphores. Data moves between devices by JAX's collectives and lax.ppermute only.
A program may use at most 64 MiB of HBM per device.

v0:
```python
import jax
import jax.numpy as jnp
import numpy as np
from jax import lax
from jax.experimental import pallas as pl
from jax.experimental.pallas import tpu as pltpu
from jax.sharding import PartitionSpec as P


F32, BF16, I32 = jnp.float32, jnp.bfloat16, jnp.int32
epsilon = 1e-06

CX, CY, CZ = 8, 16, 256
BLK = CX * CY
REACH = 3
EXT = (2 * REACH + 1) * BLK
MID = REACH * BLK
WIDE = (2 * REACH + 1) * CX
STEPS = 7
ROWS = 256
SLOTS = 8
PEERS = 64


def split2(x):
    hi = x.astype(BF16)
    return hi, (x - hi.astype(F32)).astype(BF16)


SCALE = 1.6 / 63.0
TAPS = (63.0, -7.875, 1.0, -9.0 / 128.0)
CENTRE_XY, CENTRE_Z = -336.0, -21.0 / 64.0


def band_z():
    band = np.zeros((CZ, CZ), np.float64)
    for z in range(CZ):
        band[z, z] = CENTRE_Z
        for k in range(1, 5):
            for other in (z + k, z - k):
                if 0 <= other < CZ:
                    band[other, z] = TAPS[k - 1]
    return band.astype(jnp.bfloat16)


def dot(a, b):
    return lax.dot_general(a, b, (((1,), (0,)), ((), ())), preferred_element_type=F32)


def dot_nt(a, b):
    return lax.dot_general(a, b, (((1,), (1,)), ((), ())), preferred_element_type=F32)


def one_hot(index_row, height, base=0):
    iota = lax.broadcasted_iota(I32, (height, index_row.shape[1]), 0) + base
    return jnp.where(iota == index_row, 1.0, 0.0).astype(BF16)


TRACES, WAVELET, OWNER, CELL, SOURCE_OWNER, SOURCE_CELL, TABLE = 0, 7, 14, 15, 16, 17, 24


def prep_kernel(table, out, words, padded):
    own_f = table[OWNER : OWNER + 1]
    own = own_f.astype(I32)
    column = jnp.broadcast_to(own_f, (128, ROWS)).T
    column = jnp.concatenate([column, column], axis=1)
    first = lax.broadcasted_iota(I32, (ROWS, ROWS), 0)
    second = lax.broadcasted_iota(I32, (ROWS, ROWS), 1)
    same = (column == jnp.broadcast_to(own_f, (ROWS, ROWS))) & (first < second)
    rank = jnp.sum(jnp.where(same, 1.0, 0.0), axis=0, keepdims=True).astype(I32)
    half = SLOTS // 2
    low = rank < half
    place = own * half + jnp.where(low, rank, rank - half)
    hot_low = one_hot(jnp.where(low, place, -1), PEERS * half)
    hot_high = one_hot(jnp.where(low, -1, place), PEERS * half)
    hot = jnp.concatenate([hot_low, hot_high], axis=1)
    for t in range(1, STEPS):
        words[t - 1 : t, :] = table[TRACES + t : TRACES + t + 1]
    words[6:7, :] = table[CELL : CELL + 1]
    words[7:8, :] = jnp.zeros((1, ROWS), F32)
    rest = words[...]
    total = None
    for _ in range(3):
        piece = rest.astype(BF16)
        rest = rest - piece.astype(F32)
        wide = jnp.concatenate([piece.astype(F32)] * 8, axis=0)
        empty = jnp.zeros_like(wide)
        both = jnp.concatenate(
            [jnp.concatenate([wide, empty], axis=1), jnp.concatenate([empty, wide], axis=1)], axis=0
        ).astype(BF16)
        part = dot_nt(hot, both)
        total = part if total is None else total + part
    edge = 16
    padded[0:edge, :] = jnp.zeros((edge, 128), F32)
    padded[edge + ROWS : edge + ROWS + edge, :] = jnp.zeros((edge, 128), F32)
    padded[edge : edge + ROWS, :] = total
    group = lax.broadcasted_iota(I32, (ROWS, 128), 1) % 64 // 8
    result = jnp.zeros((ROWS, 128), F32)
    for j in range(2 * REACH + 1):
        start = edge + half * (j - REACH)
        result = jnp.where(group == j, padded[start : start + ROWS, :], result)
    out[...] = result


def widen_courant(pieces, wide, me):
    wide[0:64, :] = jnp.zeros((64, CZ), F32)
    wide[EXT - 64 : EXT, :] = jnp.zeros((64, CZ), F32)
    wide[MID : MID + BLK, :] = pieces[0][...].reshape(BLK, CZ)
    _, below, above, lower, upper = pieces

    def inside(k):
        return jnp.where((me + k >= 0) & (me + k < PEERS), 1.0, 0.0)

    half = BLK // 2
    wide[half:BLK, :] = lower[0 : CX // 2].reshape(half, CZ) * inside(-3)
    wide[BLK : 2 * BLK, :] = lower[CX // 2 :].reshape(BLK, CZ) * inside(-2)
    wide[2 * BLK : MID, :] = below[...].reshape(BLK, CZ) * (SCALE * inside(-1))
    wide[MID + BLK : MID + 2 * BLK, :] = above[...].reshape(BLK, CZ) * (SCALE * inside(1))
    wide[MID + 2 * BLK : MID + 3 * BLK, :] = upper[0:CX].reshape(BLK, CZ) * inside(2)
    wide[MID + 3 * BLK : MID + 3 * BLK + half, :] = upper[CX:].reshape(half, CZ) * inside(3)


def clear_rims(field):
    rim = jnp.zeros((WIDE, 2, 8, 128), F32)
    field[:, :, 0:8, :] = rim
    field[:, :, 24:32, :] = rim


def laplace_xy(field, x, half):
    centre = field[pl.ds(x, CX), half, 8:24, :]
    out = CENTRE_XY * centre
    for k in range(1, 5):
        pairs = field[pl.ds(x + k, CX), half, 8:24, :] + field[pl.ds(x - k, CX), half, 8:24, :]
        pairs = pairs + field[pl.ds(x, CX), half, 8 + k : 24 + k, :]
        pairs = pairs + field[pl.ds(x, CX), half, 8 - k : 24 - k, :]
        out = out + TAPS[k - 1] * pairs
    return out


def rows_at(x, base=0):
    return pl.ds(pl.multiple_of(base + x * CY, 64), BLK)


def store_split(high, low, slot, x, half, value):
    hi, lo = split2(value.reshape(BLK, 128))
    at = rows_at(x)
    lanes = slice(half * 128, half * 128 + 128)
    high[slot, at, lanes], low[slot, at, lanes] = hi, lo


def over_chunks(beyond, chunk):
    def step(i, carry):
        chunk(REACH * CX - beyond + CX * i)
        return carry

    lax.fori_loop(0, beyond // 4 + 1, step, 0)


def join_kernel(courant, below, above, lower, upper):
    lower[0 : CX // 2] = below[CX // 2 :] * SCALE
    lower[CX // 2 :] = courant[...]
    upper[0:CX] = courant[...]
    upper[CX:] = above[0 : CX // 2] * SCALE


def source_places():
    bases, at = [], 0
    for t in range(STEPS):
        reach = 24 - 4 * t
        bases.append(at - (MID - reach * CY))
        at += (2 * reach + CX) * CY
    return bases


def station_places():
    spans, bases, at = {}, {}, 0
    for t in range(1, STEPS):
        reach = 4 * (t - 1)
        spans[t] = (MID - reach * CY, MID + BLK + reach * CY)
        bases[t] = at - spans[t][0]
        at += spans[t][1] - spans[t][0]
    return spans, bases


def inject_kernel(table, got, sources, stations, masks):
    me = lax.axis_index("space")
    cells = table[SOURCE_CELL : SOURCE_CELL + 1].astype(I32)
    line = (table[SOURCE_OWNER : SOURCE_OWNER + 1].astype(I32) - me + REACH) * BLK + (cells >> 8)
    hot_z = one_hot(cells & 255, CZ)
    for block in range(2 * REACH + 1):
        masks[block * BLK : (block + 1) * BLK, :] = one_hot(line, BLK, block * BLK)
    bases = source_places()
    for t in range(STEPS):
        reach = 24 - 4 * t
        rows = (2 * reach + CX) * CY
        first = MID - reach * CY
        at = bases[t] + first
        hi, lo = split2(table[WAVELET + t : WAVELET + t + 1])
        mask = masks[first : first + rows, :]
        sources[at : at + rows, :] = dot_nt(mask * hi, hot_z) + dot_nt(mask * lo, hot_z)
    slots = got[...].T
    spans, bases = station_places()
    for block in range(2 * REACH + 1):
        words = jnp.concatenate(
            [slots[block * 8 : block * 8 + 8, :], slots[64 + block * 8 : 72 + block * 8, :]], axis=1
        )
        cells = words[6:7, :].astype(I32)
        mask = one_hot(cells >> 8, BLK)
        hot_z = one_hot(cells & 255, CZ)
        places, his, los = [], [], []
        for t in range(1, STEPS):
            lower = max(spans[t][0], block * BLK)
            upper = min(spans[t][1], block * BLK + BLK)
            if lower < upper:
                hi, lo = split2(words[t - 1 : t, :])
                wanted = mask[lower - block * BLK : upper - block * BLK]
                places.append((bases[t] + lower, upper - lower))
                his.append(wanted * hi)
                los.append(wanted * lo)
        value = dot_nt(jnp.concatenate(his, axis=0), hot_z) + dot_nt(jnp.concatenate(los, axis=0), hot_z)
        at = 0
        for place, rows in places:
            stations[place : place + rows, :] = value[at : at + rows]
            at += rows


def field_kernel(*refs):
    pieces, refs = refs[:5], refs[5:]
    sources, stations, band = refs[:3]
    keep, send, norms = refs[3:6]
    wide, rim_a, rim_b, field_a, field_b, high, low, drive, total, part = refs[6:]
    me = lax.axis_index("space")
    member = lax.axis_index("batch")
    halves = [slice(0, 128), slice(128, 256)]

    def along(slot, x):
        at = rows_at(x)
        return dot(high[slot, at, :], band[...]) + dot(low[slot, at, :], band[...])

    bases = source_places()
    widen_courant(pieces, wide, me)
    clear_rims(rim_a)
    clear_rims(rim_b)
    rims = (rim_a, rim_b)

    def begin(x):
        for half, lanes in enumerate(halves):
            value = sources[rows_at(x), lanes].reshape(CX, CY, 128)
            rim_a[pl.ds(x, CX), half, 8:24, :] = value
            store_split(high, low, 0, x, half, value)

    over_chunks(24, begin)
    for t in range(1, STEPS):
        now, other, slot = rims[(t - 1) % 2], rims[t % 2], (t - 1) % 2

        def chunk(x, now=now, other=other, slot=slot, t=t):
            at = rows_at(x)
            z_part = along(slot, x)
            for half in range(2):
                part[half] = laplace_xy(now, x, half)
            for half, lanes in enumerate(halves):
                lap = part[half] + z_part[:, lanes].reshape(CX, CY, 128)
                step = wide[at, lanes].reshape(CX, CY, 128) * lap
                step = step + sources[rows_at(x, bases[t]), lanes].reshape(CX, CY, 128)
                drive[t - 1, at, lanes] = step.reshape(BLK, 128)
                if t < STEPS - 1:
                    new = 2.0 * now[pl.ds(x, CX), half, 8:24, :] + step
                    if t > 1:
                        new = new - other[pl.ds(x, CX), half, 8:24, :]
                    other[pl.ds(x, CX), half, 8:24, :] = new
                    store_split(high, low, 1 - slot, x, half, new)

        over_chunks(24 - 4 * t, chunk)

    _, bases = station_places()
    fields = (field_a, field_b)

    def begin_back(x):
        at = rows_at(x)
        for half, lanes in enumerate(halves):
            value = stations[rows_at(x, bases[6]), lanes].reshape(CX, CY, 128)
            field_a[pl.ds(x, CX), half] = value
            value = value * wide[at, lanes].reshape(CX, CY, 128)
            rim_a[pl.ds(x, CX), half, 8:24, :] = value
            store_split(high, low, 0, x, half, value)

    over_chunks(20, begin_back)

    def gather(field, t, first):
        for half, lanes in enumerate(halves):
            term = field[REACH * CX : REACH * CX + CX, half].reshape(BLK, 128)
            term = term * drive[t - 1, MID : MID + BLK, lanes]
            total[:, lanes] = term if first else total[:, lanes] + term

    gather(field_a, 6, True)
    for t in range(STEPS - 2, 0, -1):
        n = STEPS - 2 - t
        now, other, slot = fields[n % 2], fields[(n + 1) % 2], n % 2
        source, target = rims[slot], rims[1 - slot]

        def chunk(x, now=now, other=other, slot=slot, source=source, target=target, t=t, n=n):
            at = rows_at(x)
            z_part = along(slot, x)
            for half in range(2):
                part[half] = laplace_xy(source, x, half)
            for half, lanes in enumerate(halves):
                new = part[half] + z_part[:, lanes].reshape(CX, CY, 128)
                new = new + stations[rows_at(x, bases[t]), lanes].reshape(CX, CY, 128)
                new = new + 2.0 * now[pl.ds(x, CX), half]
                if n > 0:
                    new = new - other[pl.ds(x, CX), half]
                other[pl.ds(x, CX), half] = new
                if t > 1:
                    new = new * wide[at, lanes].reshape(CX, CY, 128)
                    target[pl.ds(x, CX), half, 8:24, :] = new
                    store_split(high, low, 1 - slot, x, half, new)

        over_chunks(4 * (t - 1), chunk)
        gather(other, t, False)
    gradient = total[...].reshape(CX, CY, CZ)
    squares = jnp.sum(jnp.sum(gradient * gradient, axis=0), axis=0, keepdims=True)
    norm = jnp.sum(squares, axis=1, keepdims=True)
    front, back = gradient[:, 0:8, :], gradient[:, 8:16, :]
    keep[...] = jnp.where(member == 0, front, back)
    send[...] = jnp.where(member == 0, back, front)
    norms[...] = jnp.broadcast_to(norm, (8, 128))


def finish_kernel(keep, other, norms, update, share):
    sums = jnp.sum(norms[...], axis=0, keepdims=True)
    cells = float(PEERS * BLK * CZ)
    mean_first = sums[0:1, 0:1] / cells
    mean_second = sums[0:1, 64:65] / cells
    scale = jnp.sqrt((mean_first + mean_second) / 2.0 + epsilon)
    update[...] = (keep[...] + other[...]) / scale.reshape(1, 1, 1)
    ratio = (mean_first + epsilon) / (mean_first + mean_second + 2.0 * epsilon)
    share[...] = jnp.broadcast_to(ratio, (1, 128))


VM = pl.BlockSpec(memory_space=pltpu.VMEM)


def call(kernel, outs, scratch, *args, flops=0, limit=4 << 20):
    size = sum(int(np.prod(a.shape)) * 4 for a in args)
    return pl.pallas_call(
        kernel,
        out_shape=outs,
        in_specs=[VM] * len(args),
        out_specs=jax.tree.map(lambda _: VM, outs),
        scratch_shapes=scratch,
        cost_estimate=pl.CostEstimate(flops=flops, bytes_accessed=size, transcendentals=0),
        compiler_params=pltpu.CompilerParams(vmem_limit_bytes=limit),
    )(*args)


def shape(*dims, dtype=F32):
    return jax.ShapeDtypeStruct(dims, dtype)


def body(courant, wavelet, source_owner, source_cell, traces, station_owner, station_cell):
    def shift(value, k):
        return lax.ppermute(value, "space", [(i, (i + k) % PEERS) for i in range(PEERS)])

    singles = [station_owner.reshape(1, ROWS), station_cell, source_owner, source_cell]
    table = [jnp.transpose(traces[0]), jnp.transpose(wavelet[0])] + [v.astype(F32) for v in singles]
    table = jnp.concatenate(table + [jnp.zeros((TABLE - 18, ROWS), F32)], axis=0)
    slab = courant * SCALE
    scratch = [pltpu.VMEM((8, ROWS), F32), pltpu.VMEM((ROWS + 32, 128), F32)]
    sent = call(prep_kernel, shape(ROWS, 128), scratch, table, flops=10**8)
    below, above = shift(courant, 1), shift(courant, -1)
    taller = shape(CX + CX // 2, CY, CZ)
    lower, upper = call(join_kernel, (taller, taller), [], slab, below, above)
    pieces = [slab, below, above, shift(lower, 2), shift(upper, -2)]
    got = lax.all_to_all(sent.reshape(PEERS, 4, 128), "space", split_axis=0, concat_axis=0, tiled=True)
    sources, stations = call(
        inject_kernel,
        (shape(28 * BLK, CZ), shape(21 * BLK, CZ)),
        [pltpu.VMEM((EXT, CZ), BF16)],
        table,
        got.reshape(ROWS, 128),
        flops=4 * 10**9,
        limit=12 << 20,
    )
    keep, send, mine = call(
        field_kernel,
        (shape(CX, 8, CZ), shape(CX, 8, CZ), shape(8, 128)),
        [pltpu.VMEM((EXT, CZ), F32)]
        + [pltpu.VMEM((WIDE, 2, 32, 128), F32)] * 2
        + [pltpu.VMEM((WIDE, 2, CY, 128), F32)] * 2
        + [pltpu.VMEM((2, EXT, CZ), BF16)] * 2
        + [pltpu.VMEM((STEPS - 1, EXT, CZ), F32), pltpu.VMEM((BLK, CZ), F32)]
        + [pltpu.VMEM((2, CX, CY, 128), F32)],
        *pieces,
        sources,
        stations,
        jnp.asarray(band_z()),
        flops=4 * 10**9,
        limit=30 << 20,
    )
    swap = [(0, 1), (1, 0)]
    theirs = lax.ppermute(mine, "batch", swap)
    other = lax.ppermute(send, "batch", swap)
    lanes = lax.broadcasted_iota(I32, (8, 128), 1) < 64
    row = jnp.where(lanes == (lax.axis_index("batch") == 0), mine, theirs)
    partial = jnp.broadcast_to(row[0:1][None], (PEERS, 1, 128))
    norms = lax.all_to_all(partial, "space", split_axis=0, concat_axis=0, tiled=True)
    update, share = call(
        finish_kernel, (shape(CX, 8, CZ), shape(1, 128)), [], keep, other, norms.reshape(PEERS, 128)
    )
    return update, share[0, 0:1]


def solution(mesh):
    placed = (
        P("space", None, None),
        P("batch", None, None),
        P("batch", None),
        P("batch", None),
        P("batch", "space", None),
        P("batch", "space", None),
        P("batch", "space"),
    )
    return jax.shard_map(
        body,
        mesh=mesh,
        in_specs=placed,
        out_specs=(P("space", "batch", None), P()),
        check_vma=False,
    )
```

profile of v0, /device:TPU:1, one launch (start us, length us, event | category | flops | bytes accessed | tf_op | source)
XLA Modules:
  0.0 63.3 jit_solution(1736275837803200663)
XLA Ops:
  0.6 2.7 %collective-permute-start = (f32[8,16,256]{2,1,0:T(8,128)}, f32[8,16,256]{2,1,0:T(8,128)S(1)}, u32[]{:S(2)}, u32[]{:S(2)}) collective-permute-start(f32[8,16,256]{2,1,0:T(8,128)} %param.8), channel_id=1, source_target_pairs={{0,1},{1,2},{2,3},{3,4},{4,5},{5,6},{6,7},{7,8},{8,9},{9,10},{10,1... | collective-permute-start | bytes 393224 | tf_op jit(solution)/shard_map/ppermute | solution.py:362
  3.3 0.0 collective-permute-start.1
  3.3 0.7 %convert_bitcast_fusion = f32[1,256]{1,0:T(1,128)S(1)} fusion(s32[1,256,1]{1,2,0:T(1,128)} %param.13), kind=kLoop, calls=%fused_computation.5 | loop fusion | flops 256 | bytes 2048 | tf_op jit(solution)/shard_map/convert_element_type | solution.py:365
  4.0 0.7 %convert_element_type.25 = f32[1,256]{1,0:T(1,128)S(1)} convert(s32[1,256]{1,0:T(1,128)} %param.14) | non-fusion elementwise | flops 256 | bytes 2048 | tf_op jit(solution)/shard_map/convert_element_type | solution.py:365
  4.7 0.7 %convert_element_type.26 = f32[1,256]{1,0:T(1,128)S(1)} convert(s32[1,256]{1,0:T(1,128)} %param.10) | non-fusion elementwise | flops 256 | bytes 2048 | tf_op jit(solution)/shard_map/convert_element_type | solution.py:365
  5.3 0.7 %convert_element_type.27 = f32[1,256]{1,0:T(1,128)S(1)} convert(s32[1,256]{1,0:T(1,128)} %param.11) | non-fusion elementwise | flops 256 | bytes 2048 | tf_op jit(solution)/shard_map/convert_element_type | solution.py:365
  6.0 0.7 %copy_bitcast_fusion = (f32[7,256]{1,0:T(8,128)S(1)}, f32[7,256]{1,0:T(8,128)S(1)}) fusion(f32[1,256,7]{1,0,2:T(1,128)} %param.9, f32[1,256,7]{1,0,2:T(1,128)} %param.12), kind=kLoop, calls=%fused_computation.1 | loop fusion | bytes 28672 | tf_op jit(solution)/shard_map/transpose | solution.py:365
  6.7 0.1 concatenate.3.table
  6.8 1.1 %shard_map.96 = f32[256,128]{1,0:T(8,128)} custom-call(f32[24,256]{1,0:T(8,128)S(1)} %concatenate.3.table), custom_call_target="tpu_custom_call" | custom-call | flops 100000000 | bytes 24576 | tf_op jit(solution)/shard_map/pallas_call | solution.py:345
  8.0 10.1 %all-to-all-start = ((f32[64,4,128]{2,1,0:T(4,128)}), f32[64,4,128]{2,1,0:T(4,128)S(1)}, u32[]{:S(2)}, u32[]{:S(2)}) async-start(f32[64,4,128]{2,1,0:T(4,128)} %bitcast.3), calls=%async_computation | async-start | bytes 262144 | tf_op jit(solution)/shard_map/all_to_all | solution.py:374
  18.1 0.9 %broadcast_multiply_fusion.courant.refs_0_ = f32[8,16,256]{2,1,0:T(8,128)S(1)} fusion(f32[8,16,256]{2,1,0:T(8,128)} %param.8), kind=kLoop, calls=%fused_computation | loop fusion | flops 32768 | bytes 262144 | tf_op jit(solution)/shard_map/mul | solution.py:367
  19.0 0.0 collective-permute-done.1.above.refs_2_
  19.1 1.4 %collective-permute-start.2 = (f32[12,16,256]{2,1,0:T(8,128)S(1)}, f32[12,16,256]{2,1,0:T(8,128)S(1)}, u32[]{:S(2)}, u32[]{:S(2)}) collective-permute-start(f32[12,16,256]{2,1,0:T(8,128)S(1)} %get-tuple-element.11), channel_id=1, source_target_pairs={{0,2},{1,3},{2,4},{3,5},{4,6},{5,7},{6,8},{7,9},{8,10},{9,11},{10,... | collective-permute-start | bytes 589832 | tf_op jit(solution)/shard_map/ppermute | solution.py:362
  20.5 4.6 %collective-permute-start.3 = (f32[12,16,256]{2,1,0:T(8,128)S(1)}, f32[12,16,256]{2,1,0:T(8,128)S(1)}, u32[]{:S(2)}, u32[]{:S(2)}) collective-permute-start(f32[12,16,256]{2,1,0:T(8,128)S(1)} %get-tuple-element.12), channel_id=1, source_target_pairs={{0,62},{1,63},{2,0},{3,1},{4,2},{5,3},{6,4},{7,5},{8,6},{9,7},{10,... | collective-permute-start | bytes 589832 | tf_op jit(solution)/shard_map/ppermute | solution.py:362
  25.1 1.5 %all-to-all-done = f32[64,4,128]{2,1,0:T(4,128)S(1)} async-done(((f32[64,4,128]{2,1,0:T(4,128)}), f32[64,4,128]{2,1,0:T(4,128)S(1)}, u32[]{:S(2)}, u32[]{:S(2)}) %all-to-all-start) | async-done | bytes 131104 | tf_op jit(solution)/shard_map/all_to_all | solution.py:374
  26.6 2.9 %shard_map.97 = (f32[3584,256]{1,0:T(8,128)S(1)}, f32[2688,256]{1,0:T(8,128)S(1)}) custom-call(f32[24,256]{1,0:T(8,128)S(1)} %concatenate.3.table, f32[256,128]{1,0:T(8,128)S(1)} %bitcast.18), custom_call_target="tpu_custom_call" | custom-call | flops 4000000000 | bytes 155648 | tf_op jit(solution)/shard_map/pallas_call | solution.py:345
  29.5 0.7 %collective-permute-done.2.refs_3_ = f32[12,16,256]{2,1,0:T(8,128)S(1)} collective-permute-done((f32[12,16,256]{2,1,0:T(8,128)S(1)}, f32[12,16,256]{2,1,0:T(8,128)S(1)}, u32[]{:S(2)}, u32[]{:S(2)}) %collective-permute-start.2) | collective-permute-done | bytes 196640 | tf_op jit(solution)/shard_map/ppermute | solution.py:362
  30.1 0.4 collective-permute-done.3.refs_4_
  30.5 10.0 %shard_map.98 = (f32[8,8,256]{2,1,0:T(8,128)S(1)}, f32[8,8,256]{2,1,0:T(8,128)S(1)}, f32[8,128]{1,0:T(8,128)S(1)}) custom-call(f32[8,16,256]{2,1,0:T(8,128)S(1)} %broadcast_multiply_fusion.courant.refs_0_, f32[8,16,256]{2,1,0:T(8,128)S(1)} %collective-permute-done.below.refs_1_, f32[8,16,256]{2,1,0:T(8,128)S(1)} %collective-permute-done.1.above.refs_2_, ...), custom_call_target="tpu_custom_call" | custom-call | flops 4000000000 | bytes 7471104 | tf_op jit(solution)/shard_map/pallas_call | solution.py:345
  40.5 2.7 %collective-permute-start.5 = (f32[8,128]{1,0:T(8,128)S(1)}, f32[8,128]{1,0:T(8,128)S(1)}, u32[]{:S(2)}, u32[]{:S(2)}) collective-permute-start(f32[8,128]{1,0:T(8,128)S(1)} %get-tuple-element.17), channel_id=1, source_target_pairs={{0,64},{64,0},{1,65},{65,1},{2,66},{66,2},{3,67},{67,3},{4,68},{68... | collective-permute-start | bytes 12296 | tf_op jit(solution)/shard_map/ppermute | solution.py:401
  43.2 0.3 collective-permute-start.4
  43.5 1.0 %collective-permute-done.5 = f32[8,128]{1,0:T(8,128)S(1)} collective-permute-done((f32[8,128]{1,0:T(8,128)S(1)}, f32[8,128]{1,0:T(8,128)S(1)}, u32[]{:S(2)}, u32[]{:S(2)}) %collective-permute-start.5) | collective-permute-done | bytes 4128 | tf_op jit(solution)/shard_map/ppermute | solution.py:401
  44.5 18.0 %all_to_all.10 = f32[64,1,128]{2,1,0:T(1,128)S(1)} all-to-all(f32[64,1,128]{2,1,0:T(1,128)S(1)} %broadcast_in_dim.13), channel_id=1, replica_groups=mesh['batch'=2,'space'=64] {'space'}, dimensions={0} | all-to-all | bytes 65536 | tf_op jit(solution)/shard_map/all_to_all | solution.py:406
  62.5 0.8 %shard_map.99 = (f32[8,8,256]{2,1,0:T(8,128)}, f32[1,128]{1,0:T(1,128)}) custom-call(f32[8,8,256]{2,1,0:T(8,128)S(1)} %get-tuple-element.15.keep, f32[8,8,256]{2,1,0:T(8,128)S(1)} %collective-permute-done.4.other, f32[64,128]{1,0:T(8,128)S(1)} %bitcast.17), custom_call_target="tpu_custom_call" | custom-call | bytes 163840 | tf_op jit(solution)/shard_map/pallas_call | solution.py:345
  (10 shorter events, 0.1 us)
Async XLA Ops:
  0.6 18.4 %collective-permute-start = (f32[8,16,256]{2,1,0:T(8,128)}, f32[8,16,256]{2,1,0:T(8,128)S(1)}, u32[]{:S(2)}, u32[]{:S(2)}) collective-permute-start(f32[8,16,256]{2,1,0:T(8,128)} %param.8), channel_id=1, source_target_pairs={{0,1},{1,2},{2,3},{3,4},{4,5},{5,6},{6,7},{7,8},{8,9},{9,10},{10,1... | collective-permute-start | bytes 393224 | tf_op jit(solution)/shard_map/ppermute | solution.py:362
  3.3 15.7 %collective-permute-start.1 = (f32[8,16,256]{2,1,0:T(8,128)}, f32[8,16,256]{2,1,0:T(8,128)S(1)}, u32[]{:S(2)}, u32[]{:S(2)}) collective-permute-start(f32[8,16,256]{2,1,0:T(8,128)} %param.8), channel_id=1, source_target_pairs={{0,63},{1,0},{2,1},{3,2},{4,3},{5,4},{6,5},{7,6},{8,7},{9,8},{10,9... | collective-permute-start | bytes 393224 | tf_op jit(solution)/shard_map/ppermute | solution.py:362
  8.0 18.6 %all-to-all-start = ((f32[64,4,128]{2,1,0:T(4,128)}), f32[64,4,128]{2,1,0:T(4,128)S(1)}, u32[]{:S(2)}, u32[]{:S(2)}) async-start(f32[64,4,128]{2,1,0:T(4,128)} %bitcast.3), calls=%async_computation | async-start | bytes 262144 | tf_op jit(solution)/shard_map/all_to_all | solution.py:374
  19.1 11.1 %collective-permute-start.2 = (f32[12,16,256]{2,1,0:T(8,128)S(1)}, f32[12,16,256]{2,1,0:T(8,128)S(1)}, u32[]{:S(2)}, u32[]{:S(2)}) collective-permute-start(f32[12,16,256]{2,1,0:T(8,128)S(1)} %get-tuple-element.11), channel_id=1, source_target_pairs={{0,2},{1,3},{2,4},{3,5},{4,6},{5,7},{6,8},{7,9},{8,10},{9,11},{10,... | collective-permute-start | bytes 589832 | tf_op jit(solution)/shard_map/ppermute | solution.py:362
  20.5 10.0 %collective-permute-start.3 = (f32[12,16,256]{2,1,0:T(8,128)S(1)}, f32[12,16,256]{2,1,0:T(8,128)S(1)}, u32[]{:S(2)}, u32[]{:S(2)}) collective-permute-start(f32[12,16,256]{2,1,0:T(8,128)S(1)} %get-tuple-element.12), channel_id=1, source_target_pairs={{0,62},{1,63},{2,0},{3,1},{4,2},{5,3},{6,4},{7,5},{8,6},{9,7},{10,... | collective-permute-start | bytes 589832 | tf_op jit(solution)/shard_map/ppermute | solution.py:362
  26.6 3.9 %copy-start = (bf16[256,256]{1,0:T(8,128)(2,1)S(1)}, bf16[256,256]{1,0:T(8,128)(2,1)}, u32[]{:S(2)}) copy-start(bf16[256,256]{1,0:T(8,128)(2,1)} %constant.16.clone.refs_7_) | copy-start | bytes 393220
  40.5 4.0 %collective-permute-start.5 = (f32[8,128]{1,0:T(8,128)S(1)}, f32[8,128]{1,0:T(8,128)S(1)}, u32[]{:S(2)}, u32[]{:S(2)}) collective-permute-start(f32[8,128]{1,0:T(8,128)S(1)} %get-tuple-element.17), channel_id=1, source_target_pairs={{0,64},{64,0},{1,65},{65,1},{2,66},{66,2},{3,67},{67,3},{4,68},{68... | collective-permute-start | bytes 12296 | tf_op jit(solution)/shard_map/ppermute | solution.py:401
  43.2 19.3 %collective-permute-start.4 = (f32[8,8,256]{2,1,0:T(8,128)S(1)}, f32[8,8,256]{2,1,0:T(8,128)S(1)}, u32[]{:S(2)}, u32[]{:S(2)}) collective-permute-start(f32[8,8,256]{2,1,0:T(8,128)S(1)} %get-tuple-element.16), channel_id=1, source_target_pairs={{0,64},{64,0},{1,65},{65,1},{2,66},{66,2},{3,67},{67,3},{4,68},{68... | collective-permute-start | bytes 196616 | tf_op jit(solution)/shard_map/ppermute | solution.py:402
where the time goes:
time: 63.6 us; the launch traced here: 63.3 us
  starting transfers between devices  21.7 us (34%)
  blocking collectives  18 us (28%)
  Pallas kernels  14.8 us (23%)
  other arithmetic  3.65 us (6%)
  waiting for transfers between devices  3.49 us (5%)
  local copies, waits for them, and re-layouts  0.86 us (1%)
  between operations  0.7 us (1%)
    all_to_all x1, blocking collectives, body(): lax.all_to_all(partial, 'space', split_axis=0, concat_axis=0, tiled=True)  18 us
    pallas_call x5, Pallas kernels, call(): pl.pallas_call(kernel, out_shape=outs, in_specs=[VM] * len(args), out_spe...  14.8 us
    all_to_all x1, starting transfers between devices, body(): lax.all_to_all(sent.reshape(PEERS, 4, 128), 'space', split_axis=0, concat...  10.1 us
    ppermute x4, starting transfers between devices, shift(): lax.ppermute(value, 'space', [(i, (i + k) % PEERS) for i in range(PEERS)])  8.69 us
    ppermute x1, starting transfers between devices, body(): theirs = lax.ppermute(mine, 'batch', swap)  2.73 us
    convert_element_type x4, other arithmetic, body(): v.astype(F32)  2.72 us
    all_to_all x1, waiting for transfers between devices, body(): lax.all_to_all(sent.reshape(PEERS, 4, 128), 'space', split_axis=0, concat...  1.47 us
  transfers between devices with their start and end apart: 7, of which 4 were waited for; matrix products, arithmetic and copies ran while one was open for 7% of the time, Pallas kernels for 6%

commit v1 on v0

--- a/solution.py
+++ b/solution.py
@@ -56,12 +56,11 @@
     return jnp.where(iota == index_row, 1.0, 0.0).astype(BF16)
 
 
-TRACES, WAVELET, OWNER, CELL, SOURCE_OWNER, SOURCE_CELL, TABLE = 0, 7, 14, 15, 16, 17, 24
-
-
-def prep_kernel(table, out, words, padded):
-    own_f = table[OWNER : OWNER + 1]
-    own = own_f.astype(I32)
+def prep_kernel(traces, owner, cell, courant, out, front, back, words, padded):
+    front[...] = courant[0 : CX // 2]
+    back[...] = courant[CX // 2 :]
+    own = owner[...]
+    own_f = own.astype(F32)
     column = jnp.broadcast_to(own_f, (128, ROWS)).T
     column = jnp.concatenate([column, column], axis=1)
     first = lax.broadcasted_iota(I32, (ROWS, ROWS), 0)
@@ -75,8 +74,8 @@
     hot_high = one_hot(jnp.where(low, -1, place), PEERS * half)
     hot = jnp.concatenate([hot_low, hot_high], axis=1)
     for t in range(1, STEPS):
-        words[t - 1 : t, :] = table[TRACES + t : TRACES + t + 1]
-    words[6:7, :] = table[CELL : CELL + 1]
+        words[t - 1 : t, :] = traces[t]
+    words[6:7, :] = cell[...].astype(F32)
     words[7:8, :] = jnp.zeros((1, ROWS), F32)
     rest = words[...]
     total = None
@@ -105,19 +104,14 @@
 def widen_courant(pieces, wide, me):
     wide[0:64, :] = jnp.zeros((64, CZ), F32)
     wide[EXT - 64 : EXT, :] = jnp.zeros((64, CZ), F32)
-    wide[MID : MID + BLK, :] = pieces[0][...].reshape(BLK, CZ)
-    _, below, above, lower, upper = pieces
-
-    def inside(k):
-        return jnp.where((me + k >= 0) & (me + k < PEERS), 1.0, 0.0)
-
-    half = BLK // 2
-    wide[half:BLK, :] = lower[0 : CX // 2].reshape(half, CZ) * inside(-3)
-    wide[BLK : 2 * BLK, :] = lower[CX // 2 :].reshape(BLK, CZ) * inside(-2)
-    wide[2 * BLK : MID, :] = below[...].reshape(BLK, CZ) * (SCALE * inside(-1))
-    wide[MID + BLK : MID + 2 * BLK, :] = above[...].reshape(BLK, CZ) * (SCALE * inside(1))
-    wide[MID + 2 * BLK : MID + 3 * BLK, :] = upper[0:CX].reshape(BLK, CZ) * inside(2)
-    wide[MID + 3 * BLK : MID + 3 * BLK + half, :] = upper[CX:].reshape(half, CZ) * inside(3)
+    wide[MID : MID + BLK, :] = pieces[0][...].reshape(BLK, CZ) * SCALE
+    for k in range(1, REACH + 1):
+        rows = BLK // 2 if k == REACH else BLK
+        below, above = pieces[2 * k - 1], pieces[2 * k]
+        has_below = jnp.where(me >= k, SCALE, 0.0)
+        has_above = jnp.where(me + k < PEERS, SCALE, 0.0)
+        wide[MID - (k - 1) * BLK - rows : MID - (k - 1) * BLK, :] = below[...].reshape(rows, CZ) * has_below
+        wide[MID + k * BLK : MID + k * BLK + rows, :] = above[...].reshape(rows, CZ) * has_above
 
 
 def clear_rims(field):
@@ -126,41 +120,47 @@
     field[:, :, 24:32, :] = rim
 
 
-def laplace_xy(field, x, half):
-    centre = field[pl.ds(x, CX), half, 8:24, :]
+def laplace_xy(field, x, half, rows):
+    centre = field[pl.ds(x, rows), half, 8:24, :]
     out = CENTRE_XY * centre
     for k in range(1, 5):
-        pairs = field[pl.ds(x + k, CX), half, 8:24, :] + field[pl.ds(x - k, CX), half, 8:24, :]
-        pairs = pairs + field[pl.ds(x, CX), half, 8 + k : 24 + k, :]
-        pairs = pairs + field[pl.ds(x, CX), half, 8 - k : 24 - k, :]
+        pairs = field[pl.ds(x + k, rows), half, 8:24, :] + field[pl.ds(x - k, rows), half, 8:24, :]
+        pairs = pairs + field[pl.ds(x, rows), half, 8 + k : 24 + k, :]
+        pairs = pairs + field[pl.ds(x, rows), half, 8 - k : 24 - k, :]
         out = out + TAPS[k - 1] * pairs
     return out
 
 
-def rows_at(x, base=0):
-    return pl.ds(pl.multiple_of(base + x * CY, 64), BLK)
-
-
-def store_split(high, low, slot, x, half, value):
-    hi, lo = split2(value.reshape(BLK, 128))
-    at = rows_at(x)
+def rows_at(x, rows, base=0):
+    return pl.ds(pl.multiple_of(base + x * CY, 64), rows * CY)
+
+
+def store_split(high, low, slot, x, half, value, rows):
+    hi, lo = split2(value.reshape(rows * CY, 128))
+    at = rows_at(x, rows)
     lanes = slice(half * 128, half * 128 + 128)
     high[slot, at, lanes], low[slot, at, lanes] = hi, lo
 
 
+TRIP = {56: 8, 48: 16, 40: 20, 32: 16, 24: 24, 16: 16, 8: 8}
+
+
 def over_chunks(beyond, chunk):
+    total = 2 * beyond + CX
+    rows = TRIP[total]
+
     def step(i, carry):
-        chunk(REACH * CX - beyond + CX * i)
+        chunk(REACH * CX - beyond + rows * i, rows)
         return carry
 
-    lax.fori_loop(0, beyond // 4 + 1, step, 0)
-
-
-def join_kernel(courant, below, above, lower, upper):
-    lower[0 : CX // 2] = below[CX // 2 :] * SCALE
-    lower[CX // 2 :] = courant[...]
-    upper[0:CX] = courant[...]
-    upper[CX:] = above[0 : CX // 2] * SCALE
+    if rows == total:
+        step(0, 0)
+    else:
+        lax.fori_loop(0, total // rows, step, 0)
+
+
+def pieces_of(rows):
+    return [(i, min(CX, rows - i)) for i in range(0, rows, CX)]
 
 
 def source_places():
@@ -182,10 +182,10 @@
     return spans, bases
 
 
-def inject_kernel(table, got, sources, stations, masks):
+def inject_kernel(wavelet, owner, cell, got, sources, stations, masks):
     me = lax.axis_index("space")
-    cells = table[SOURCE_CELL : SOURCE_CELL + 1].astype(I32)
-    line = (table[SOURCE_OWNER : SOURCE_OWNER + 1].astype(I32) - me + REACH) * BLK + (cells >> 8)
+    cells = cell[...]
+    line = (owner[...] - me + REACH) * BLK + (cells >> 8)
     hot_z = one_hot(cells & 255, CZ)
     for block in range(2 * REACH + 1):
         masks[block * BLK : (block + 1) * BLK, :] = one_hot(line, BLK, block * BLK)
@@ -195,7 +195,7 @@
         rows = (2 * reach + CX) * CY
         first = MID - reach * CY
         at = bases[t] + first
-        hi, lo = split2(table[WAVELET + t : WAVELET + t + 1])
+        hi, lo = split2(wavelet[t])
         mask = masks[first : first + rows, :]
         sources[at : at + rows, :] = dot_nt(mask * hi, hot_z) + dot_nt(mask * lo, hot_z)
     slots = got[...].T
@@ -225,17 +225,17 @@
 
 
 def field_kernel(*refs):
-    pieces, refs = refs[:5], refs[5:]
+    pieces, refs = refs[:7], refs[7:]
     sources, stations, band = refs[:3]
     keep, send, norms = refs[3:6]
-    wide, rim_a, rim_b, field_a, field_b, high, low, drive, total, part = refs[6:]
+    wide, rim_a, rim_b, field_a, field_b, high, low, drive, total, part, z_part = refs[6:]
     me = lax.axis_index("space")
     member = lax.axis_index("batch")
     halves = [slice(0, 128), slice(128, 256)]
 
-    def along(slot, x):
-        at = rows_at(x)
-        return dot(high[slot, at, :], band[...]) + dot(low[slot, at, :], band[...])
+    def along(slot, x, rows):
+        at = rows_at(x, rows)
+        z_part[0 : rows * CY, :] = dot(high[slot, at, :], band[...]) + dot(low[slot, at, :], band[...])
 
     bases = source_places()
     widen_courant(pieces, wide, me)
@@ -243,46 +243,52 @@
     clear_rims(rim_b)
     rims = (rim_a, rim_b)
 
-    def begin(x):
+    def begin(x, rows):
         for half, lanes in enumerate(halves):
-            value = sources[rows_at(x), lanes].reshape(CX, CY, 128)
-            rim_a[pl.ds(x, CX), half, 8:24, :] = value
-            store_split(high, low, 0, x, half, value)
+            value = sources[rows_at(x, rows), lanes].reshape(rows, CY, 128)
+            rim_a[pl.ds(x, rows), half, 8:24, :] = value
+            store_split(high, low, 0, x, half, value, rows)
 
     over_chunks(24, begin)
     for t in range(1, STEPS):
         now, other, slot = rims[(t - 1) % 2], rims[t % 2], (t - 1) % 2
 
-        def chunk(x, now=now, other=other, slot=slot, t=t):
-            at = rows_at(x)
-            z_part = along(slot, x)
-            for half in range(2):
-                part[half] = laplace_xy(now, x, half)
-            for half, lanes in enumerate(halves):
-                lap = part[half] + z_part[:, lanes].reshape(CX, CY, 128)
-                step = wide[at, lanes].reshape(CX, CY, 128) * lap
-                step = step + sources[rows_at(x, bases[t]), lanes].reshape(CX, CY, 128)
-                drive[t - 1, at, lanes] = step.reshape(BLK, 128)
-                if t < STEPS - 1:
-                    new = 2.0 * now[pl.ds(x, CX), half, 8:24, :] + step
-                    if t > 1:
-                        new = new - other[pl.ds(x, CX), half, 8:24, :]
-                    other[pl.ds(x, CX), half, 8:24, :] = new
-                    store_split(high, low, 1 - slot, x, half, new)
+        def chunk(x0, count, now=now, other=other, slot=slot, t=t):
+            along(slot, x0, count)
+            for i, rows in pieces_of(count):
+                for half in range(2):
+                    part[half, i : i + rows] = laplace_xy(now, x0 + i, half, rows)
+            for i, rows in pieces_of(count):
+                x = x0 + i
+                at = rows_at(x, rows)
+                for half, lanes in enumerate(halves):
+                    lap = part[half, i : i + rows]
+                    lap = lap + z_part[i * CY : (i + rows) * CY, lanes].reshape(rows, CY, 128)
+                    step = wide[at, lanes].reshape(rows, CY, 128) * lap
+                    step = step + sources[rows_at(x, rows, bases[t]), lanes].reshape(rows, CY, 128)
+                    drive[t - 1, at, lanes] = step.reshape(rows * CY, 128)
+                    if t < STEPS - 1:
+                        new = 2.0 * now[pl.ds(x, rows), half, 8:24, :] + step
+                        if t > 1:
+                            new = new - other[pl.ds(x, rows), half, 8:24, :]
+                        other[pl.ds(x, rows), half, 8:24, :] = new
+                        store_split(high, low, 1 - slot, x, half, new, rows)
 
         over_chunks(24 - 4 * t, chunk)
 
     _, bases = station_places()
     fields = (field_a, field_b)
 
-    def begin_back(x):
-        at = rows_at(x)
-        for half, lanes in enumerate(halves):
-            value = stations[rows_at(x, bases[6]), lanes].reshape(CX, CY, 128)
-            field_a[pl.ds(x, CX), half] = value
-            value = value * wide[at, lanes].reshape(CX, CY, 128)
-            rim_a[pl.ds(x, CX), half, 8:24, :] = value
-            store_split(high, low, 0, x, half, value)
+    def begin_back(x0, count):
+        for i, rows in pieces_of(count):
+            x = x0 + i
+            at = rows_at(x, rows)
+            for half, lanes in enumerate(halves):
+                value = stations[rows_at(x, rows, bases[6]), lanes].reshape(rows, CY, 128)
+                field_a[pl.ds(x, rows), half] = value
+                value = value * wide[at, lanes].reshape(rows, CY, 128)
+                rim_a[pl.ds(x, rows), half, 8:24, :] = value
+                store_split(high, low, 0, x, half, value, rows)
 
     over_chunks(20, begin_back)
 
@@ -298,22 +304,26 @@
         now, other, slot = fields[n % 2], fields[(n + 1) % 2], n % 2
         source, target = rims[slot], rims[1 - slot]
 
-        def chunk(x, now=now, other=other, slot=slot, source=source, target=target, t=t, n=n):
-            at = rows_at(x)
-            z_part = along(slot, x)
-            for half in range(2):
-                part[half] = laplace_xy(source, x, half)
-            for half, lanes in enumerate(halves):
-                new = part[half] + z_part[:, lanes].reshape(CX, CY, 128)
-                new = new + stations[rows_at(x, bases[t]), lanes].reshape(CX, CY, 128)
-                new = new + 2.0 * now[pl.ds(x, CX), half]
-                if n > 0:
-                    new = new - other[pl.ds(x, CX), half]
-                other[pl.ds(x, CX), half] = new
-                if t > 1:
-                    new = new * wide[at, lanes].reshape(CX, CY, 128)
-                    target[pl.ds(x, CX), half, 8:24, :] = new
-                    store_split(high, low, 1 - slot, x, half, new)
+        def chunk(x0, count, now=now, other=other, slot=slot, source=source, target=target, t=t, n=n):
+            along(slot, x0, count)
+            for i, rows in pieces_of(count):
+                for half in range(2):
+                    part[half, i : i + rows] = laplace_xy(source, x0 + i, half, rows)
+            for i, rows in pieces_of(count):
+                x = x0 + i
+                at = rows_at(x, rows)
+                for half, lanes in enumerate(halves):
+                    new = part[half, i : i + rows]
+                    new = new + z_part[i * CY : (i + rows) * CY, lanes].reshape(rows, CY, 128)
+                    new = new + stations[rows_at(x, rows, bases[t]), lanes].reshape(rows, CY, 128)
+                    new = new + 2.0 * now[pl.ds(x, rows), half]
+                    if n > 0:
+                        new = new - other[pl.ds(x, rows), half]
+                    other[pl.ds(x, rows), half] = new
+                    if t > 1:
+                        new = new * wide[at, lanes].reshape(rows, CY, 128)
+                        target[pl.ds(x, rows), half, 8:24, :] = new
+                        store_split(high, low, 1 - slot, x, half, new, rows)
 
         over_chunks(4 * (t - 1), chunk)
         gather(other, t, False)
@@ -361,22 +371,30 @@
     def shift(value, k):
         return lax.ppermute(value, "space", [(i, (i + k) % PEERS) for i in range(PEERS)])
 
-    singles = [station_owner.reshape(1, ROWS), station_cell, source_owner, source_cell]
-    table = [jnp.transpose(traces[0]), jnp.transpose(wavelet[0])] + [v.astype(F32) for v in singles]
-    table = jnp.concatenate(table + [jnp.zeros((TABLE - 18, ROWS), F32)], axis=0)
-    slab = courant * SCALE
-    scratch = [pltpu.VMEM((8, ROWS), F32), pltpu.VMEM((ROWS + 32, 128), F32)]
-    sent = call(prep_kernel, shape(ROWS, 128), scratch, table, flops=10**8)
-    below, above = shift(courant, 1), shift(courant, -1)
-    taller = shape(CX + CX // 2, CY, CZ)
-    lower, upper = call(join_kernel, (taller, taller), [], slab, below, above)
-    pieces = [slab, below, above, shift(lower, 2), shift(upper, -2)]
+    half_slab = shape(CX // 2, CY, CZ)
+    sent, front, back = call(
+        prep_kernel,
+        (shape(ROWS, 128), half_slab, half_slab),
+        [pltpu.VMEM((8, ROWS), F32), pltpu.VMEM((ROWS + 32, 128), F32)],
+        jnp.transpose(traces, (2, 0, 1)),
+        station_owner.reshape(1, ROWS),
+        station_cell,
+        courant,
+        flops=10**8,
+        limit=None,
+    )
+    pieces = [courant]
+    for k in range(1, REACH + 1):
+        below, above = (back, front) if k == REACH else (courant, courant)
+        pieces += [shift(below, k), shift(above, -k)]
     got = lax.all_to_all(sent.reshape(PEERS, 4, 128), "space", split_axis=0, concat_axis=0, tiled=True)
     sources, stations = call(
         inject_kernel,
         (shape(28 * BLK, CZ), shape(21 * BLK, CZ)),
         [pltpu.VMEM((EXT, CZ), BF16)],
-        table,
+        jnp.transpose(wavelet, (2, 0, 1)),
+        source_owner,
+        source_cell,
         got.reshape(ROWS, 128),
         flops=4 * 10**9,
         limit=12 << 20,
@@ -389,7 +407,7 @@
         + [pltpu.VMEM((WIDE, 2, CY, 128), F32)] * 2
         + [pltpu.VMEM((2, EXT, CZ), BF16)] * 2
         + [pltpu.VMEM((STEPS - 1, EXT, CZ), F32), pltpu.VMEM((BLK, CZ), F32)]
-        + [pltpu.VMEM((2, CX, CY, 128), F32)],
+        + [pltpu.VMEM((2, 24, CY, 128), F32), pltpu.VMEM((24 * CY, CZ), F32)],
         *pieces,
         sources,
         stations,

time: 63.6 us -> 61.5 us (0.967)
  starting transfers between devices: 21.7 us -> 26.8 us
  other arithmetic: 3.65 us -> 0.01 us
  blocking collectives: 18 us -> 15.5 us
  waiting for transfers between devices: 3.49 us -> 1.73 us
  local copies, waits for them, and re-layouts: 0.86 us -> 2.09 us
    ppermute x4 -> x6, starting transfers between devices: 8.69 us -> 12.9 us  [shift(): lax.ppermute(value, 'space', [(i, (i + k) % PEERS) for i in range(PEERS)])]
    convert_element_type x4 -> x0, other arithmetic: 2.72 us -> none  [body(): v.astype(F32)]
    all_to_all x1, blocking collectives: 18 us -> 15.5 us  [body(): lax.all_to_all(partial, 'space', split_axis=0, concat_axis=0, tiled=True)]
    unnamed x2 -> x10, local copies, waits for them, and re-layouts: 0.01 us -> 2.06 us
    all_to_all x1, waiting for transfers between devices: 1.47 us -> 0.01 us  [body(): lax.all_to_all(sent.reshape(PEERS, 4, 128), 'space', split_axis=0, concat...]
    mul x1 -> x0, other arithmetic: 0.92 us -> none  [body(): slab = courant * SCALE]
    all_to_all x1, starting transfers between devices: 10.1 us -> 10.9 us  [body(): lax.all_to_all(sent.reshape(PEERS, 4, 128), 'space', split_axis=0, concat...]
    transpose x1 -> x0, local copies, waits for them, and re-layouts: 0.71 us -> none  [body(): jnp.transpose(wavelet[0])]
  transfers between devices with their start and end apart: 7 -> 9, of which waited for: 4 -> 2; matrix products, arithmetic and copies ran while one was open for 7% -> 0% of each run, Pallas kernels for 6% -> 5%
where the time goes in v1:
time: 61.5 us; the launch traced here: 61.2 us
  starting transfers between devices  26.8 us (44%)
  blocking collectives  15.5 us (25%)
  Pallas kernels  14.4 us (23%)
  local copies, waits for them, and re-layouts  2.09 us (3%)
  waiting for transfers between devices  1.73 us (3%)
  between operations  0.72 us (1%)
    all_to_all x1, blocking collectives, body(): lax.all_to_all(partial, 'space', split_axis=0, concat_axis=0, tiled=True)  15.5 us
    pallas_call x4, Pallas kernels, call(): pl.pallas_call(kernel, out_shape=outs, in_specs=[VM] * len(args), out_spe...  14.4 us
    ppermute x6, starting transfers between devices, shift(): lax.ppermute(value, 'space', [(i, (i + k) % PEERS) for i in range(PEERS)])  12.9 us
    all_to_all x1, starting transfers between devices, body(): lax.all_to_all(sent.reshape(PEERS, 4, 128), 'space', split_axis=0, concat...  10.9 us
    ppermute x1, starting transfers between devices, body(): theirs = lax.ppermute(mine, 'batch', swap)  2.44 us
    unnamed x10, local copies, waits for them, and re-layouts  2.06 us
  transfers between devices with their start and end apart: 9, of which 2 were waited for; matrix products, arithmetic and copies ran while one was open for 0% of the time, Pallas kernels for 5%

profile of v1, /device:TPU:1, one launch (start us, length us, event | category | flops | bytes accessed | tf_op | source)
XLA Modules:
  0.0 61.2 jit_solution(275794048822655387)
XLA Ops:
  0.6 2.1 %shard_map.95 = (f32[256,128]{1,0:T(8,128)}, f32[4,16,256]{2,1,0:T(8,128)}, f32[4,16,256]{2,1,0:T(8,128)}) custom-call(f32[7,1,256]{2,1,0:T(1,128)} %bitcast.14, s32[1,256]{1,0:T(1,128)} %bitcast.15, s32[1,256]{1,0:T(1,128)} %cell.2, f32[8,16,256]{2,1,0:T(8,128)} %refs_0_.1), custom_call_target="tpu_custom_call" | custom-call | flops 100000000 | bytes 140288 | tf_op jit(solution)/shard_map/pallas_call | solution.py:355
  2.8 10.9 %all-to-all-start = ((f32[64,4,128]{2,1,0:T(4,128)}), f32[64,4,128]{2,1,0:T(4,128)S(1)}, u32[]{:S(2)}, u32[]{:S(2)}) async-start(f32[64,4,128]{2,1,0:T(4,128)} %bitcast.13), calls=%async_computation | async-start | bytes 262144 | tf_op jit(solution)/shard_map/all_to_all | solution.py:390
  13.7 1.7 %collective-permute-start.4 = (f32[4,16,256]{2,1,0:T(8,128)}, f32[4,16,256]{2,1,0:T(8,128)S(1)}, u32[]{:S(2)}, u32[]{:S(2)}) collective-permute-start(f32[4,16,256]{2,1,0:T(8,128)} %get-tuple-element.12), channel_id=1, source_target_pairs={{0,3},{1,4},{2,5},{3,6},{4,7},{5,8},{6,9},{7,10},{8,11},{9,12},{10... | collective-permute-start | bytes 196616 | tf_op jit(solution)/shard_map/ppermute | solution.py:372
  15.4 1.2 %collective-permute-start = (f32[8,16,256]{2,1,0:T(8,128)}, f32[8,16,256]{2,1,0:T(8,128)S(1)}, u32[]{:S(2)}, u32[]{:S(2)}) collective-permute-start(f32[8,16,256]{2,1,0:T(8,128)} %refs_0_.1), channel_id=1, source_target_pairs={{0,1},{1,2},{2,3},{3,4},{4,5},{5,6},{6,7},{7,8},{8,9},{9,10},{10,1... | collective-permute-start | bytes 393224 | tf_op jit(solution)/shard_map/ppermute | solution.py:372
  16.6 0.0 collective-permute-start.1
  16.6 1.2 %collective-permute-start.2 = (f32[8,16,256]{2,1,0:T(8,128)}, f32[8,16,256]{2,1,0:T(8,128)S(1)}, u32[]{:S(2)}, u32[]{:S(2)}) collective-permute-start(f32[8,16,256]{2,1,0:T(8,128)} %refs_0_.1), channel_id=1, source_target_pairs={{0,2},{1,3},{2,4},{3,5},{4,6},{5,7},{6,8},{7,9},{8,10},{9,11},{10,... | collective-permute-start | bytes 393224 | tf_op jit(solution)/shard_map/ppermute | solution.py:372
  17.8 4.5 %collective-permute-start.3 = (f32[8,16,256]{2,1,0:T(8,128)}, f32[8,16,256]{2,1,0:T(8,128)S(1)}, u32[]{:S(2)}, u32[]{:S(2)}) collective-permute-start(f32[8,16,256]{2,1,0:T(8,128)} %refs_0_.1), channel_id=1, source_target_pairs={{0,62},{1,63},{2,0},{3,1},{4,2},{5,3},{6,4},{7,5},{8,6},{9,7},{10,... | collective-permute-start | bytes 393224 | tf_op jit(solution)/shard_map/ppermute | solution.py:372
  22.3 0.7 %collective-permute-done.4.refs_5_ = f32[4,16,256]{2,1,0:T(8,128)S(1)} collective-permute-done((f32[4,16,256]{2,1,0:T(8,128)}, f32[4,16,256]{2,1,0:T(8,128)S(1)}, u32[]{:S(2)}, u32[]{:S(2)}) %collective-permute-start.4) | collective-permute-done | bytes 65568 | tf_op jit(solution)/shard_map/ppermute | solution.py:372
  23.0 4.3 %collective-permute-start.5 = (f32[4,16,256]{2,1,0:T(8,128)}, f32[4,16,256]{2,1,0:T(8,128)S(1)}, u32[]{:S(2)}, u32[]{:S(2)}) collective-permute-start(f32[4,16,256]{2,1,0:T(8,128)} %get-tuple-element.13), channel_id=1, source_target_pairs={{0,61},{1,62},{2,63},{3,0},{4,1},{5,2},{6,3},{7,4},{8,5},{9,6},{10... | collective-permute-start | bytes 196616 | tf_op jit(solution)/shard_map/ppermute | solution.py:372
  27.3 0.0 all-to-all-done
  27.3 0.7 %copy-done.1 = f32[1,256,7]{1,0,2:T(1,128)S(1)} copy-done((f32[1,256,7]{1,0,2:T(1,128)S(1)}, f32[1,256,7]{1,0,2:T(1,128)}, u32[]{:S(2)}) %copy-start.1) | copy-done | bytes 7192
  28.0 0.7 %copy-done.2 = s32[1,256]{1,0:T(1,128)S(1)} copy-done((s32[1,256]{1,0:T(1,128)S(1)}, s32[1,256]{1,0:T(1,128)}, u32[]{:S(2)}) %copy-start.2) | copy-done | bytes 1048
  28.7 0.7 %copy-done.3 = s32[1,256]{1,0:T(1,128)S(1)} copy-done((s32[1,256]{1,0:T(1,128)S(1)}, s32[1,256]{1,0:T(1,128)}, u32[]{:S(2)}) %copy-start.3) | copy-done | bytes 1048
  29.4 2.9 %shard_map.96 = (f32[3584,256]{1,0:T(8,128)S(1)}, f32[2688,256]{1,0:T(8,128)S(1)}) custom-call(f32[7,1,256]{2,1,0:T(1,128)S(1)} %bitcast.12, s32[1,256]{1,0:T(1,128)S(1)} %copy-done.2, s32[1,256]{1,0:T(1,128)S(1)} %copy-done.3, f32[256,128]{1,0:T(8,128)S(1)} %bitcast.11), custom_call_target="tpu_custom_call" | custom-call | flops 4000000000 | bytes 140288 | tf_op jit(solution)/shard_map/pallas_call | solution.py:355
  32.3 0.0 collective-permute-done.5.refs_6_
  32.3 0.0 collective-permute-done.refs_1_
  32.3 0.0 collective-permute-done.1.refs_2_
  32.3 0.0 collective-permute-done.3.refs_4_
  32.4 8.7 %shard_map.97 = (f32[8,8,256]{2,1,0:T(8,128)S(1)}, f32[8,8,256]{2,1,0:T(8,128)S(1)}, f32[8,128]{1,0:T(8,128)S(1)}) custom-call(f32[8,16,256]{2,1,0:T(8,128)S(1)} %copy-done, f32[8,16,256]{2,1,0:T(8,128)S(1)} %collective-permute-done.refs_1_, f32[8,16,256]{2,1,0:T(8,128)S(1)} %collective-permute-done.1.refs_2_, ...), custom_call_target="tpu_custom_call" | custom-call | flops 4000000000 | bytes 7471104 | tf_op jit(solution)/shard_map/pallas_call | solution.py:355
  41.0 2.4 %collective-permute-start.7 = (f32[8,128]{1,0:T(8,128)S(1)}, f32[8,128]{1,0:T(8,128)S(1)}, u32[]{:S(2)}, u32[]{:S(2)}) collective-permute-start(f32[8,128]{1,0:T(8,128)S(1)} %get-tuple-element.19), channel_id=1, source_target_pairs={{0,64},{64,0},{1,65},{65,1},{2,66},{66,2},{3,67},{67,3},{4,68},{68... | collective-permute-start | bytes 12296 | tf_op jit(solution)/shard_map/ppermute | solution.py:419
  43.5 0.5 collective-permute-start.6
  44.0 1.0 %collective-permute-done.7 = f32[8,128]{1,0:T(8,128)S(1)} collective-permute-done((f32[8,128]{1,0:T(8,128)S(1)}, f32[8,128]{1,0:T(8,128)S(1)}, u32[]{:S(2)}, u32[]{:S(2)}) %collective-permute-start.7) | collective-permute-done | bytes 4128 | tf_op jit(solution)/shard_map/ppermute | solution.py:419
  45.0 15.5 %all_to_all.10 = f32[64,1,128]{2,1,0:T(1,128)S(1)} all-to-all(f32[64,1,128]{2,1,0:T(1,128)S(1)} %broadcast_in_dim.9), channel_id=1, replica_groups=mesh['batch'=2,'space'=64] {'space'}, dimensions={0} | all-to-all | bytes 65536 | tf_op jit(solution)/shard_map/all_to_all | solution.py:424
  60.5 0.8 %shard_map.98 = (f32[8,8,256]{2,1,0:T(8,128)}, f32[1,128]{1,0:T(1,128)}) custom-call(f32[8,8,256]{2,1,0:T(8,128)S(1)} %get-tuple-element.17.keep, f32[8,8,256]{2,1,0:T(8,128)S(1)} %collective-permute-done.6.other, f32[64,128]{1,0:T(8,128)S(1)} %bitcast.10), custom_call_target="tpu_custom_call" | custom-call | bytes 163840 | tf_op jit(solution)/shard_map/pallas_call | solution.py:355
  (13 shorter events, 0.1 us)
Async XLA Ops:
  2.8 24.6 %all-to-all-start = ((f32[64,4,128]{2,1,0:T(4,128)}), f32[64,4,128]{2,1,0:T(4,128)S(1)}, u32[]{:S(2)}, u32[]{:S(2)}) async-start(f32[64,4,128]{2,1,0:T(4,128)} %bitcast.13), calls=%async_computation | async-start | bytes 262144 | tf_op jit(solution)/shard_map/all_to_all | solution.py:390
  13.7 9.3 %collective-permute-start.4 = (f32[4,16,256]{2,1,0:T(8,128)}, f32[4,16,256]{2,1,0:T(8,128)S(1)}, u32[]{:S(2)}, u32[]{:S(2)}) collective-permute-start(f32[4,16,256]{2,1,0:T(8,128)} %get-tuple-element.12), channel_id=1, source_target_pairs={{0,3},{1,4},{2,5},{3,6},{4,7},{5,8},{6,9},{7,10},{8,11},{9,12},{10... | collective-permute-start | bytes 196616 | tf_op jit(solution)/shard_map/ppermute | solution.py:372
  15.4 16.9 %collective-permute-start = (f32[8,16,256]{2,1,0:T(8,128)}, f32[8,16,256]{2,1,0:T(8,128)S(1)}, u32[]{:S(2)}, u32[]{:S(2)}) collective-permute-start(f32[8,16,256]{2,1,0:T(8,128)} %refs_0_.1), channel_id=1, source_target_pairs={{0,1},{1,2},{2,3},{3,4},{4,5},{5,6},{6,7},{7,8},{8,9},{9,10},{10,1... | collective-permute-start | bytes 393224 | tf_op jit(solution)/shard_map/ppermute | solution.py:372
  16.6 15.7 %collective-permute-start.1 = (f32[8,16,256]{2,1,0:T(8,128)}, f32[8,16,256]{2,1,0:T(8,128)S(1)}, u32[]{:S(2)}, u32[]{:S(2)}) collective-permute-start(f32[8,16,256]{2,1,0:T(8,128)} %refs_0_.1), channel_id=1, source_target_pairs={{0,63},{1,0},{2,1},{3,2},{4,3},{5,4},{6,5},{7,6},{8,7},{9,8},{10,9... | collective-permute-start | bytes 393224 | tf_op jit(solution)/shard_map/ppermute | solution.py:372
  16.6 15.7 %collective-permute-start.2 = (f32[8,16,256]{2,1,0:T(8,128)}, f32[8,16,256]{2,1,0:T(8,128)S(1)}, u32[]{:S(2)}, u32[]{:S(2)}) collective-permute-start(f32[8,16,256]{2,1,0:T(8,128)} %refs_0_.1), channel_id=1, source_target_pairs={{0,2},{1,3},{2,4},{3,5},{4,6},{5,7},{6,8},{7,9},{8,10},{9,11},{10,... | collective-permute-start | bytes 393224 | tf_op jit(solution)/shard_map/ppermute | solution.py:372
  17.8 14.6 %collective-permute-start.3 = (f32[8,16,256]{2,1,0:T(8,128)}, f32[8,16,256]{2,1,0:T(8,128)S(1)}, u32[]{:S(2)}, u32[]{:S(2)}) collective-permute-start(f32[8,16,256]{2,1,0:T(8,128)} %refs_0_.1), channel_id=1, source_target_pairs={{0,62},{1,63},{2,0},{3,1},{4,2},{5,3},{6,4},{7,5},{8,6},{9,7},{10,... | collective-permute-start | bytes 393224 | tf_op jit(solution)/shard_map/ppermute | solution.py:372
  23.0 9.3 %collective-permute-start.5 = (f32[4,16,256]{2,1,0:T(8,128)}, f32[4,16,256]{2,1,0:T(8,128)S(1)}, u32[]{:S(2)}, u32[]{:S(2)}) collective-permute-start(f32[4,16,256]{2,1,0:T(8,128)} %get-tuple-element.13), channel_id=1, source_target_pairs={{0,61},{1,62},{2,63},{3,0},{4,1},{5,2},{6,3},{7,4},{8,5},{9,6},{10... | collective-permute-start | bytes 196616 | tf_op jit(solution)/shard_map/ppermute | solution.py:372
  27.3 0.7 %copy-start.1 = (f32[1,256,7]{1,0,2:T(1,128)S(1)}, f32[1,256,7]{1,0,2:T(1,128)}, u32[]{:S(2)}) copy-start(f32[1,256,7]{1,0,2:T(1,128)} %param.9) | copy-start | bytes 21508
  28.0 0.7 %copy-start.2 = (s32[1,256]{1,0:T(1,128)S(1)}, s32[1,256]{1,0:T(1,128)}, u32[]{:S(2)}) copy-start(s32[1,256]{1,0:T(1,128)} %owner.1) | copy-start | bytes 3076
  28.7 0.7 %copy-start.3 = (s32[1,256]{1,0:T(1,128)S(1)}, s32[1,256]{1,0:T(1,128)}, u32[]{:S(2)}) copy-start(s32[1,256]{1,0:T(1,128)} %cell.3) | copy-start | bytes 3076
  29.4 2.9 %copy-start = (f32[8,16,256]{2,1,0:T(8,128)S(1)}, f32[8,16,256]{2,1,0:T(8,128)}, u32[]{:S(2)}) copy-start(f32[8,16,256]{2,1,0:T(8,128)} %refs_0_.1) | copy-start | bytes 393220
  29.4 3.0 %copy-start.4 = (bf16[256,256]{1,0:T(8,128)(2,1)S(1)}, bf16[256,256]{1,0:T(8,128)(2,1)}, u32[]{:S(2)}) copy-start(bf16[256,256]{1,0:T(8,128)(2,1)} %constant.12.clone.refs_9_) | copy-start | bytes 393220
  41.0 4.0 %collective-permute-start.7 = (f32[8,128]{1,0:T(8,128)S(1)}, f32[8,128]{1,0:T(8,128)S(1)}, u32[]{:S(2)}, u32[]{:S(2)}) collective-permute-start(f32[8,128]{1,0:T(8,128)S(1)} %get-tuple-element.19), channel_id=1, source_target_pairs={{0,64},{64,0},{1,65},{65,1},{2,66},{66,2},{3,67},{67,3},{4,68},{68... | collective-permute-start | bytes 12296 | tf_op jit(solution)/shard_map/ppermute | solution.py:419
  43.5 17.0 %collective-permute-start.6 = (f32[8,8,256]{2,1,0:T(8,128)S(1)}, f32[8,8,256]{2,1,0:T(8,128)S(1)}, u32[]{:S(2)}, u32[]{:S(2)}) collective-permute-start(f32[8,8,256]{2,1,0:T(8,128)S(1)} %get-tuple-element.18), channel_id=1, source_target_pairs={{0,64},{64,0},{1,65},{65,1},{2,66},{66,2},{3,67},{67,3},{4,68},{68... | collective-permute-start | bytes 196616 | tf_op jit(solution)/shard_map/ppermute | solution.py:420

commit v2 on v1

--- a/solution.py
+++ b/solution.py
@@ -56,9 +56,7 @@
     return jnp.where(iota == index_row, 1.0, 0.0).astype(BF16)
 
 
-def prep_kernel(traces, owner, cell, courant, out, front, back, words, padded):
-    front[...] = courant[0 : CX // 2]
-    back[...] = courant[CX // 2 :]
+def prep_kernel(traces, owner, cell, out, words, padded):
     own = owner[...]
     own_f = own.astype(F32)
     column = jnp.broadcast_to(own_f, (128, ROWS)).T
@@ -105,13 +103,18 @@
     wide[0:64, :] = jnp.zeros((64, CZ), F32)
     wide[EXT - 64 : EXT, :] = jnp.zeros((64, CZ), F32)
     wide[MID : MID + BLK, :] = pieces[0][...].reshape(BLK, CZ) * SCALE
-    for k in range(1, REACH + 1):
-        rows = BLK // 2 if k == REACH else BLK
-        below, above = pieces[2 * k - 1], pieces[2 * k]
-        has_below = jnp.where(me >= k, SCALE, 0.0)
-        has_above = jnp.where(me + k < PEERS, SCALE, 0.0)
-        wide[MID - (k - 1) * BLK - rows : MID - (k - 1) * BLK, :] = below[...].reshape(rows, CZ) * has_below
-        wide[MID + k * BLK : MID + k * BLK + rows, :] = above[...].reshape(rows, CZ) * has_above
+    _, below, above, lower, upper = pieces
+
+    def inside(k):
+        return jnp.where((me + k >= 0) & (me + k < PEERS), SCALE, 0.0)
+
+    half = BLK // 2
+    wide[half:BLK, :] = lower[0 : CX // 2].reshape(half, CZ) * inside(-3)
+    wide[BLK : 2 * BLK, :] = lower[CX // 2 :].reshape(BLK, CZ) * inside(-2)
+    wide[2 * BLK : MID, :] = below[...].reshape(BLK, CZ) * inside(-1)
+    wide[MID + BLK : MID + 2 * BLK, :] = above[...].reshape(BLK, CZ) * inside(1)
+    wide[MID + 2 * BLK : MID + 3 * BLK, :] = upper[0:CX].reshape(BLK, CZ) * inside(2)
+    wide[MID + 3 * BLK : MID + 3 * BLK + half, :] = upper[CX:].reshape(half, CZ) * inside(3)
 
 
 def clear_rims(field):
@@ -142,7 +145,7 @@
     high[slot, at, lanes], low[slot, at, lanes] = hi, lo
 
 
-TRIP = {56: 8, 48: 16, 40: 20, 32: 16, 24: 24, 16: 16, 8: 8}
+TRIP = {56: 28, 48: 24, 40: 20, 32: 16, 24: 24, 16: 16, 8: 8}
 
 
 def over_chunks(beyond, chunk):
@@ -161,6 +164,13 @@
 
 def pieces_of(rows):
     return [(i, min(CX, rows - i)) for i in range(0, rows, CX)]
+
+
+def join_kernel(courant, below, above, lower, upper):
+    lower[0 : CX // 2] = below[CX // 2 :]
+    lower[CX // 2 :] = courant[...]
+    upper[0:CX] = courant[...]
+    upper[CX:] = above[0 : CX // 2]
 
 
 def source_places():
@@ -225,7 +235,7 @@
 
 
 def field_kernel(*refs):
-    pieces, refs = refs[:7], refs[7:]
+    pieces, refs = refs[:5], refs[5:]
     sources, stations, band = refs[:3]
     keep, send, norms = refs[3:6]
     wide, rim_a, rim_b, field_a, field_b, high, low, drive, total, part, z_part = refs[6:]
@@ -371,22 +381,20 @@
     def shift(value, k):
         return lax.ppermute(value, "space", [(i, (i + k) % PEERS) for i in range(PEERS)])
 
-    half_slab = shape(CX // 2, CY, CZ)
-    sent, front, back = call(
+    sent = call(
         prep_kernel,
-        (shape(ROWS, 128), half_slab, half_slab),
+        shape(ROWS, 128),
         [pltpu.VMEM((8, ROWS), F32), pltpu.VMEM((ROWS + 32, 128), F32)],
         jnp.transpose(traces, (2, 0, 1)),
         station_owner.reshape(1, ROWS),
         station_cell,
-        courant,
         flops=10**8,
         limit=None,
     )
-    pieces = [courant]
-    for k in range(1, REACH + 1):
-        below, above = (back, front) if k == REACH else (courant, courant)
-        pieces += [shift(below, k), shift(above, -k)]
+    below, above = shift(courant, 1), shift(courant, -1)
+    taller = shape(CX + CX // 2, CY, CZ)
+    lower, upper = call(join_kernel, (taller, taller), [], courant, below, above)
+    pieces = [courant, below, above, shift(lower, 2), shift(upper, -2)]
     got = lax.all_to_all(sent.reshape(PEERS, 4, 128), "space", split_axis=0, concat_axis=0, tiled=True)
     sources, stations = call(
         inject_kernel,

time: 61.5 us -> 59.3 us (0.964)
  starting transfers between devices: 26.8 us -> 21.7 us
  blocking collectives: 15.5 us -> 16.9 us
  local copies, waits for them, and re-layouts: 2.09 us -> 2.98 us
  waiting for transfers between devices: 1.73 us -> 2.49 us
    ppermute x6 -> x4, starting transfers between devices: 12.9 us -> 8.69 us  [shift(): lax.ppermute(value, 'space', [(i, (i + k) % PEERS) for i in range(PEERS)])]
    all_to_all x1, waiting for transfers between devices: 0.01 us -> 1.49 us  [body(): lax.all_to_all(sent.reshape(PEERS, 4, 128), 'space', split_axis=0, concat...]
    all_to_all x1, blocking collectives: 15.5 us -> 16.9 us  [body(): lax.all_to_all(partial, 'space', split_axis=0, concat_axis=0, tiled=True)]
    unnamed x10 -> x12, local copies, waits for them, and re-layouts: 2.06 us -> 2.96 us
    all_to_all x1, starting transfers between devices: 10.9 us -> 10.1 us  [body(): lax.all_to_all(sent.reshape(PEERS, 4, 128), 'space', split_axis=0, concat...]
    ppermute x6 -> x4, waiting for transfers between devices: 0.74 us -> 0.01 us  [shift(): lax.ppermute(value, 'space', [(i, (i + k) % PEERS) for i in range(PEERS)])]
    pallas_call x4 -> x5, Pallas kernels: 14.4 us -> 14.1 us  [call(): pl.pallas_call(kernel, out_shape=outs, in_specs=[VM] * len(args), out_spe...]
  transfers between devices with their start and end apart: 9 -> 7, of which waited for: 2 -> 2; matrix products, arithmetic and copies ran while one was open for 0% -> 0% of each run, Pallas kernels for 5% -> 8%
where the time goes in v2:
time: 59.3 us; the launch traced here: 58.9 us
  starting transfers between devices  21.7 us (37%)
  blocking collectives  16.9 us (28%)
  Pallas kernels  14.1 us (24%)
  local copies, waits for them, and re-layouts  2.98 us (5%)
  waiting for transfers between devices  2.49 us (4%)
  between operations  0.73 us (1%)
    all_to_all x1, blocking collectives, body(): lax.all_to_all(partial, 'space', split_axis=0, concat_axis=0, tiled=True)  16.9 us
    pallas_call x5, Pallas kernels, call(): pl.pallas_call(kernel, out_shape=outs, in_specs=[VM] * len(args), out_spe...  14.1 us
    all_to_all x1, starting transfers between devices, body(): lax.all_to_all(sent.reshape(PEERS, 4, 128), 'space', split_axis=0, concat...  10.1 us
    ppermute x4, starting transfers between devices, shift(): lax.ppermute(value, 'space', [(i, (i + k) % PEERS) for i in range(PEERS)])  8.69 us
    unnamed x12, local copies, waits for them, and re-layouts  2.96 us
    ppermute x1, starting transfers between devices, body(): theirs = lax.ppermute(mine, 'batch', swap)  2.73 us
    all_to_all x1, waiting for transfers between devices, body(): lax.all_to_all(sent.reshape(PEERS, 4, 128), 'space', split_axis=0, concat...  1.49 us
  transfers between devices with their start and end apart: 7, of which 2 were waited for; matrix products, arithmetic and copies ran while one was open for 0% of the time, Pallas kernels for 8%

profile of v2, /device:TPU:1, one launch (start us, length us, event | category | flops | bytes accessed | tf_op | source)
XLA Modules:
  0.0 58.9 jit_solution(14746454732458601584)
XLA Ops:
  0.6 2.7 %collective-permute-start = (f32[8,16,256]{2,1,0:T(8,128)}, f32[8,16,256]{2,1,0:T(8,128)S(1)}, u32[]{:S(2)}, u32[]{:S(2)}) collective-permute-start(f32[8,16,256]{2,1,0:T(8,128)} %refs_0_.1), channel_id=1, source_target_pairs={{0,1},{1,2},{2,3},{3,4},{4,5},{5,6},{6,7},{7,8},{8,9},{9,10},{10,1... | collective-permute-start | bytes 393224 | tf_op jit(solution)/shard_map/ppermute | solution.py:382
  3.3 0.0 collective-permute-start.1
  3.3 1.9 %shard_map.96 = f32[256,128]{1,0:T(8,128)} custom-call(f32[7,1,256]{2,1,0:T(1,128)} %bitcast.14, s32[1,256]{1,0:T(1,128)} %bitcast.15, s32[1,256]{1,0:T(1,128)} %cell.2), custom_call_target="tpu_custom_call" | custom-call | flops 100000000 | bytes 9216 | tf_op jit(solution)/shard_map/pallas_call | solution.py:365
  5.2 10.1 %all-to-all-start = ((f32[64,4,128]{2,1,0:T(4,128)}), f32[64,4,128]{2,1,0:T(4,128)S(1)}, u32[]{:S(2)}, u32[]{:S(2)}) async-start(f32[64,4,128]{2,1,0:T(4,128)} %bitcast.13), calls=%async_computation | async-start | bytes 262144 | tf_op jit(solution)/shard_map/all_to_all | solution.py:398
  15.2 0.0 collective-permute-done.below.refs_1_
  15.3 0.0 collective-permute-done.1.above.refs_2_
  15.3 0.0 copy-start
  15.3 0.9 %copy-done = f32[8,16,256]{2,1,0:T(8,128)S(1)} copy-done((f32[8,16,256]{2,1,0:T(8,128)S(1)}, f32[8,16,256]{2,1,0:T(8,128)}, u32[]{:S(2)}) %copy-start) | copy-done | bytes 131096
  16.2 1.4 %collective-permute-start.2 = (f32[12,16,256]{2,1,0:T(8,128)S(1)}, f32[12,16,256]{2,1,0:T(8,128)S(1)}, u32[]{:S(2)}, u32[]{:S(2)}) collective-permute-start(f32[12,16,256]{2,1,0:T(8,128)S(1)} %get-tuple-element.11), channel_id=1, source_target_pairs={{0,2},{1,3},{2,4},{3,5},{4,6},{5,7},{6,8},{7,9},{8,10},{9,11},{10,... | collective-permute-start | bytes 589832 | tf_op jit(solution)/shard_map/ppermute | solution.py:382
  17.6 4.6 %collective-permute-start.3 = (f32[12,16,256]{2,1,0:T(8,128)S(1)}, f32[12,16,256]{2,1,0:T(8,128)S(1)}, u32[]{:S(2)}, u32[]{:S(2)}) collective-permute-start(f32[12,16,256]{2,1,0:T(8,128)S(1)} %get-tuple-element.12), channel_id=1, source_target_pairs={{0,62},{1,63},{2,0},{3,1},{4,2},{5,3},{6,4},{7,5},{8,6},{9,7},{10,... | collective-permute-start | bytes 589832 | tf_op jit(solution)/shard_map/ppermute | solution.py:382
  22.2 1.5 %all-to-all-done = f32[64,4,128]{2,1,0:T(4,128)S(1)} async-done(((f32[64,4,128]{2,1,0:T(4,128)}), f32[64,4,128]{2,1,0:T(4,128)S(1)}, u32[]{:S(2)}, u32[]{:S(2)}) %all-to-all-start) | async-done | bytes 131104 | tf_op jit(solution)/shard_map/all_to_all | solution.py:398
  23.7 0.7 %copy-done.2 = f32[1,256,7]{1,0,2:T(1,128)S(1)} copy-done((f32[1,256,7]{1,0,2:T(1,128)S(1)}, f32[1,256,7]{1,0,2:T(1,128)}, u32[]{:S(2)}) %copy-start.2) | copy-done | bytes 7192
  24.4 0.7 %copy-done.3 = s32[1,256]{1,0:T(1,128)S(1)} copy-done((s32[1,256]{1,0:T(1,128)S(1)}, s32[1,256]{1,0:T(1,128)}, u32[]{:S(2)}) %copy-start.3) | copy-done | bytes 1048
  25.1 0.7 %copy-done.4 = s32[1,256]{1,0:T(1,128)S(1)} copy-done((s32[1,256]{1,0:T(1,128)S(1)}, s32[1,256]{1,0:T(1,128)}, u32[]{:S(2)}) %copy-start.4) | copy-done | bytes 1048
  25.8 2.9 %shard_map.97 = (f32[3584,256]{1,0:T(8,128)S(1)}, f32[2688,256]{1,0:T(8,128)S(1)}) custom-call(f32[7,1,256]{2,1,0:T(1,128)S(1)} %bitcast.12, s32[1,256]{1,0:T(1,128)S(1)} %copy-done.3, s32[1,256]{1,0:T(1,128)S(1)} %copy-done.4, f32[256,128]{1,0:T(8,128)S(1)} %bitcast.11), custom_call_target="tpu_custom_call" | custom-call | flops 4000000000 | bytes 140288 | tf_op jit(solution)/shard_map/pallas_call | solution.py:365
  28.7 0.0 collective-permute-done.2.refs_3_
  28.7 0.0 collective-permute-done.3.refs_4_
  28.7 8.5 %shard_map.98 = (f32[8,8,256]{2,1,0:T(8,128)S(1)}, f32[8,8,256]{2,1,0:T(8,128)S(1)}, f32[8,128]{1,0:T(8,128)S(1)}) custom-call(f32[8,16,256]{2,1,0:T(8,128)S(1)} %copy-done.1, f32[8,16,256]{2,1,0:T(8,128)S(1)} %collective-permute-done.below.refs_1_, f32[8,16,256]{2,1,0:T(8,128)S(1)} %collective-permute-done.1.above.refs_2_, ...), custom_call_target="tpu_custom_call" | custom-call | flops 4000000000 | bytes 7471104 | tf_op jit(solution)/shard_map/pallas_call | solution.py:365
  37.3 2.7 %collective-permute-start.5 = (f32[8,128]{1,0:T(8,128)S(1)}, f32[8,128]{1,0:T(8,128)S(1)}, u32[]{:S(2)}, u32[]{:S(2)}) collective-permute-start(f32[8,128]{1,0:T(8,128)S(1)} %get-tuple-element.17), channel_id=1, source_target_pairs={{0,64},{64,0},{1,65},{65,1},{2,66},{66,2},{3,67},{67,3},{4,68},{68... | collective-permute-start | bytes 12296 | tf_op jit(solution)/shard_map/ppermute | solution.py:427
  40.0 0.3 collective-permute-start.4
  40.2 1.0 %collective-permute-done.5 = f32[8,128]{1,0:T(8,128)S(1)} collective-permute-done((f32[8,128]{1,0:T(8,128)S(1)}, f32[8,128]{1,0:T(8,128)S(1)}, u32[]{:S(2)}, u32[]{:S(2)}) %collective-permute-start.5) | collective-permute-done | bytes 4128 | tf_op jit(solution)/shard_map/ppermute | solution.py:427
  41.3 16.9 %all_to_all.10 = f32[64,1,128]{2,1,0:T(1,128)S(1)} all-to-all(f32[64,1,128]{2,1,0:T(1,128)S(1)} %broadcast_in_dim.9), channel_id=1, replica_groups=mesh['batch'=2,'space'=64] {'space'}, dimensions={0} | all-to-all | bytes 65536 | tf_op jit(solution)/shard_map/all_to_all | solution.py:432
  58.2 0.0 collective-permute-done.4.other
  58.2 0.8 %shard_map.99 = (f32[8,8,256]{2,1,0:T(8,128)}, f32[1,128]{1,0:T(1,128)}) custom-call(f32[8,8,256]{2,1,0:T(8,128)S(1)} %get-tuple-element.15.keep, f32[8,8,256]{2,1,0:T(8,128)S(1)} %collective-permute-done.4.other, f32[64,128]{1,0:T(8,128)S(1)} %bitcast.10), custom_call_target="tpu_custom_call" | custom-call | bytes 163840 | tf_op jit(solution)/shard_map/pallas_call | solution.py:365
  (12 shorter events, 0.1 us)
Async XLA Ops:
  0.6 14.6 %collective-permute-start = (f32[8,16,256]{2,1,0:T(8,128)}, f32[8,16,256]{2,1,0:T(8,128)S(1)}, u32[]{:S(2)}, u32[]{:S(2)}) collective-permute-start(f32[8,16,256]{2,1,0:T(8,128)} %refs_0_.1), channel_id=1, source_target_pairs={{0,1},{1,2},{2,3},{3,4},{4,5},{5,6},{6,7},{7,8},{8,9},{9,10},{10,1... | collective-permute-start | bytes 393224 | tf_op jit(solution)/shard_map/ppermute | solution.py:382
  3.3 12.0 %collective-permute-start.1 = (f32[8,16,256]{2,1,0:T(8,128)}, f32[8,16,256]{2,1,0:T(8,128)S(1)}, u32[]{:S(2)}, u32[]{:S(2)}) collective-permute-start(f32[8,16,256]{2,1,0:T(8,128)} %refs_0_.1), channel_id=1, source_target_pairs={{0,63},{1,0},{2,1},{3,2},{4,3},{5,4},{6,5},{7,6},{8,7},{9,8},{10,9... | collective-permute-start | bytes 393224 | tf_op jit(solution)/shard_map/ppermute | solution.py:382
  5.2 18.6 %all-to-all-start = ((f32[64,4,128]{2,1,0:T(4,128)}), f32[64,4,128]{2,1,0:T(4,128)S(1)}, u32[]{:S(2)}, u32[]{:S(2)}) async-start(f32[64,4,128]{2,1,0:T(4,128)} %bitcast.13), calls=%async_computation | async-start | bytes 262144 | tf_op jit(solution)/shard_map/all_to_all | solution.py:398
  15.3 0.9 %copy-start = (f32[8,16,256]{2,1,0:T(8,128)S(1)}, f32[8,16,256]{2,1,0:T(8,128)}, u32[]{:S(2)}) copy-start(f32[8,16,256]{2,1,0:T(8,128)} %refs_0_.1) | copy-start | bytes 393220
  16.2 12.5 %collective-permute-start.2 = (f32[12,16,256]{2,1,0:T(8,128)S(1)}, f32[12,16,256]{2,1,0:T(8,128)S(1)}, u32[]{:S(2)}, u32[]{:S(2)}) collective-permute-start(f32[12,16,256]{2,1,0:T(8,128)S(1)} %get-tuple-element.11), channel_id=1, source_target_pairs={{0,2},{1,3},{2,4},{3,5},{4,6},{5,7},{6,8},{7,9},{8,10},{9,11},{10,... | collective-permute-start | bytes 589832 | tf_op jit(solution)/shard_map/ppermute | solution.py:382
  17.6 11.1 %collective-permute-start.3 = (f32[12,16,256]{2,1,0:T(8,128)S(1)}, f32[12,16,256]{2,1,0:T(8,128)S(1)}, u32[]{:S(2)}, u32[]{:S(2)}) collective-permute-start(f32[12,16,256]{2,1,0:T(8,128)S(1)} %get-tuple-element.12), channel_id=1, source_target_pairs={{0,62},{1,63},{2,0},{3,1},{4,2},{5,3},{6,4},{7,5},{8,6},{9,7},{10,... | collective-permute-start | bytes 589832 | tf_op jit(solution)/shard_map/ppermute | solution.py:382
  23.7 0.7 %copy-start.2 = (f32[1,256,7]{1,0,2:T(1,128)S(1)}, f32[1,256,7]{1,0,2:T(1,128)}, u32[]{:S(2)}) copy-start(f32[1,256,7]{1,0,2:T(1,128)} %param.9) | copy-start | bytes 21508
  24.4 0.7 %copy-start.3 = (s32[1,256]{1,0:T(1,128)S(1)}, s32[1,256]{1,0:T(1,128)}, u32[]{:S(2)}) copy-start(s32[1,256]{1,0:T(1,128)} %owner.1) | copy-start | bytes 3076
  25.1 0.7 %copy-start.4 = (s32[1,256]{1,0:T(1,128)S(1)}, s32[1,256]{1,0:T(1,128)}, u32[]{:S(2)}) copy-start(s32[1,256]{1,0:T(1,128)} %cell.3) | copy-start | bytes 3076
  25.8 2.9 %copy-start.1 = (f32[8,16,256]{2,1,0:T(8,128)S(1)}, f32[8,16,256]{2,1,0:T(8,128)}, u32[]{:S(2)}) copy-start(f32[8,16,256]{2,1,0:T(8,128)} %refs_0_.1) | copy-start | bytes 393220
  25.8 2.9 %copy-start.5 = (bf16[256,256]{1,0:T(8,128)(2,1)S(1)}, bf16[256,256]{1,0:T(8,128)(2,1)}, u32[]{:S(2)}) copy-start(bf16[256,256]{1,0:T(8,128)(2,1)} %constant.12.clone.refs_7_) | copy-start | bytes 393220
  37.3 4.0 %collective-permute-start.5 = (f32[8,128]{1,0:T(8,128)S(1)}, f32[8,128]{1,0:T(8,128)S(1)}, u32[]{:S(2)}, u32[]{:S(2)}) collective-permute-start(f32[8,128]{1,0:T(8,128)S(1)} %get-tuple-element.17), channel_id=1, source_target_pairs={{0,64},{64,0},{1,65},{65,1},{2,66},{66,2},{3,67},{67,3},{4,68},{68... | collective-permute-start | bytes 12296 | tf_op jit(solution)/shard_map/ppermute | solution.py:427
  40.0 18.2 %collective-permute-start.4 = (f32[8,8,256]{2,1,0:T(8,128)S(1)}, f32[8,8,256]{2,1,0:T(8,128)S(1)}, u32[]{:S(2)}, u32[]{:S(2)}) collective-permute-start(f32[8,8,256]{2,1,0:T(8,128)S(1)} %get-tuple-element.16), channel_id=1, source_target_pairs={{0,64},{64,0},{1,65},{65,1},{2,66},{66,2},{3,67},{67,3},{4,68},{68... | collective-permute-start | bytes 196616 | tf_op jit(solution)/shard_map/ppermute | solution.py:428
